TPU v7x, 256 devices: a whole 4x4x8 slice. The times are simulated.
256 devices in a mesh: row: 16 (over x, y_hi, core), col: 16 (over z, y_lo).
Axes of the slice: x: 4, y: 4 (y_hi: 2, y_lo: 2; y = y_hi * 2 + y_lo), z: 8, core: 2. Of those that a mesh axis runs over, the one named last changes fastest.
Arguments:
- panel_cols: bfloat16 [48, 4096, 512], P('col', 'row'), may hold values from -6 to 6
- inverses: bfloat16 [2, 256, 256], replicated, as said below
- trailing: bfloat16 [48, 4096, 4096], P(None, 'row', 'col'), may hold values from -6 to 6
Outputs:
- updated: bfloat16 [48, 4096, 4096], P(None, 'row', 'col')
Inputs may be any that keep to these rules, and one draw needn't show every extreme that they name: `inverses`: each of the two 256 x 256 matrices is lower triangular with a positive diagonal.
All inputs are finite; a program needn't handle non-finite values.
Results may differ from a plain program's by a relative error of at most 0.0063.
Values may be sent and summed in bfloat16 or wider, within the bound.
A program may use at most 128 MiB of HBM per device.

v0:
```python
import jax
import jax.numpy as jnp
from jax import lax
from jax.sharding import PartitionSpec as P


def broadcast(value, axis, source):
    kept = jnp.where(lax.axis_index(axis) == source, value, 0).astype(value.dtype)
    return lax.psum(kept, axis)


def shards(panel_cols, inverses, trailing):
    tile_size = panel_cols.shape[1]
    grid_rows = lax.axis_size("row")
    grid_cols = lax.axis_size("col")
    col_index = lax.axis_index("col")
    left_factor = jnp.einsum(
        "tak,bk->tab", panel_cols[:, :, :tile_size], inverses[0], preferred_element_type=jnp.float32
    ).astype(jnp.bfloat16)
    couple_tile = broadcast(left_factor[0], ("row", "col"), grid_cols)
    reduced = (
        panel_cols[:, :, tile_size:].astype(jnp.float32)
        - jnp.einsum("tak,bk->tab", left_factor, couple_tile, preferred_element_type=jnp.float32)
    ).astype(jnp.bfloat16)
    right_factor = jnp.einsum(
        "tak,bk->tab", reduced, inverses[1], preferred_element_type=jnp.float32
    ).astype(jnp.bfloat16)
    factored = jnp.concatenate([left_factor, right_factor], axis=2)
    root_row = (col_index + 2) % grid_rows
    source_tile = (col_index + 2) // grid_rows
    whole_panel = lax.all_gather(factored, "col", axis=0, tiled=True)
    key_tile = broadcast(
        lax.dynamic_index_in_dim(whole_panel, source_tile, 0, keepdims=False), "row", root_row
    )
    update_sum = jnp.einsum(
        "tak,bk->tab", whole_panel, key_tile, preferred_element_type=jnp.float32
    )
    return (trailing.astype(jnp.float32) - update_sum).astype(jnp.bfloat16)


def solution(mesh):
    in_specs = (P("col", "row", None), P(), P(None, "row", "col"))
    out_specs = P(None, "row", "col")
    return jax.shard_map(shards, mesh=mesh, in_specs=in_specs, out_specs=out_specs, check_vma=False)
```

profile of v0, /device:TPU:8, one launch (start us, length us, event | category | flops | bytes accessed | tf_op | source)
XLA Modules:
  0.0 690.4 jit_solution(11645885408623004183)
XLA Ops:
  6.5 0.0 all-reduce.3.cloned.1.call-start
  6.5 1.3 convolution_convert_fusion.1
  7.9 0.7 fusion.5
  8.5 0.0 all-reduce.3.cloned.1.call-update
  8.6 0.0 all-gather.2.cloned.1.call-start
  8.6 249.2 %all-reduce.3.cloned.1.call-done = bf16[256,256]{0,1:T(8,128)(2,1)} async-done(((bf16[256,256]{0,1:T(8,128)(2,1)}), bf16[256,256]{0,1:T(8,128)(2,1)}) %all-reduce.3.cloned.1.call-update) | async-done | bytes 131088 | tf_op jit(solution)/shard_map/psum | solution.py:9
  257.8 1.7 convolution_convert_fusion
  259.5 0.1 pad_maximum_fusion
  259.6 1.2 copy.6
  260.8 0.0 all-gather.2.cloned.1.call-update
  260.8 0.0 all-reduce.5.cloned.1.call-start
  260.9 262.1 %all-gather.2.cloned.1.call-done = bf16[48,256,512]{2,1,0:T(8,128)(2,1)} async-done(((bf16[3,256,512]{2,1,0:T(8,128)(2,1)}), bf16[48,256,512]{2,1,0:T(8,128)(2,1)}) %all-gather.2.cloned.1.call-update) | async-done | bytes 12582928 | tf_op jit(solution)/shard_map/all_gather | solution.py:31
  523.0 1.7 select_bitcast_fusion
  524.6 0.0 all-reduce.5.cloned.1.call-update
  524.7 146.6 %all-reduce.5.cloned.1.call-done = bf16[256,512]{1,0:T(8,128)(2,1)} async-done(((bf16[256,512]{1,0:T(8,128)(2,1)}), bf16[256,512]{1,0:T(8,128)(2,1)}) %all-reduce.5.cloned.1.call-update) | async-done | bytes 262160 | tf_op jit(solution)/shard_map/psum | solution.py:9
  671.2 12.6 %subtract_convert_fusion = bf16[48,256,256]{2,1,0:T(8,128)(2,1)} fusion(bf16[48,256,256]{2,1,0:T(8,128)(2,1)} %param.5, bf16[48,256,512]{2,1,0:T(8,128)(2,1)} %all-gather.2.cloned.1.call-done, bf16[256,512]{1,0:T(8,128)(2,1)} %all-reduce.5.cloned.1.call-done), kind=kOutput, calls=%fused_computation | convolution fusion | flops 3230662656 | bytes 25427968 | tf_op jit(solution)/shard_map/tak,bk->tab/dot_general | solution.py:35
Async XLA Ops:
  6.5 251.3 %all-reduce.3.cloned.1.call-start = ((), (), s32[]{:S(2)}) async-start(), calls=%async_computation | async-start | bytes 262144 | tf_op jit(solution)/shard_map/psum | solution.py:9
  8.6 514.4 %all-gather.2.cloned.1.call-start = ((), (), s32[]{:S(2)}) async-start(), calls=%async_computation.1 | async-start | bytes 13369344 | tf_op jit(solution)/shard_map/all_gather | solution.py:31
  260.8 410.4 %all-reduce.5.cloned.1.call-start = ((), (), s32[]{:S(2)}) async-start(), calls=%async_computation.2 | async-start | bytes 524288 | tf_op jit(solution)/shard_map/psum | solution.py:9
Sparse Core Ops, SparseCore 0:
  12.9 244.9 all-reduce.2
  260.9 262.0 all-gather.1
  525.6 145.6 all-reduce.4
where the time goes:
time: 692 us; the launch traced here: 690 us
  waiting for transfers between devices  658 us (95%)
  matrix products  15.6 us (2%)
  between operations  13.2 us (2%)
    psum x2, waiting for transfers between devices, broadcast(): return lax.psum(kept, axis)  396 us
    all_gather x1, waiting for transfers between devices, shards(): whole_panel = lax.all_gather(factored, 'col', axis=0, tiled=True)  262 us
  transfers between devices with their start and end apart: 3, of which 3 were waited for; matrix products, arithmetic and copies ran while one was open for 0% of the time, Pallas kernels for 0%

commit v1 on v0

v1 whole, which is shorter than its diff:
```python
import functools

import jax
import jax.numpy as jnp
from jax import lax
from jax.experimental import pallas as pl
from jax.experimental.pallas import tpu as pltpu
from jax.sharding import PartitionSpec as P

MESH = pl.DeviceIdType.MESH
TILE = 256
SHARED = 128
PIECE = 16


def times_transposed(left, right):
    return lax.dot_general(left, right, (((1,), (1,)), ((), ())), preferred_element_type=jnp.float32)


def kernel(
    panel, inverses, trailing, updated,
    own, mate, shared, sums_in, sums_out, window, pieces, couple, keys,
    ring_send, ring_recv, mate_send, mate_recv, sum_send, sum_recv,
    load_sem, piece_sem, spread_send, spread_recv, out_sem,
):
    row, col = lax.axis_index("row"), lax.axis_index("col")
    z, y = col // 2, lax.rem(col, 2)
    chip, core = row // 2, lax.rem(row, 2)
    my_piece = core * PIECE + chip * 2 + y
    mate_dev = (row, col + 1 - 2 * y)
    ring_dev = ((row, lax.rem(col + 2, 16)), (row, lax.rem(col + 14, 16)))
    plain = TILE - SHARED

    load_own = pltpu.make_async_copy(panel, own.at[z], load_sem.at[0])
    load_window = pltpu.make_async_copy(trailing, window, load_sem.at[1])
    load_own.start()
    load_window.start()

    def plane_device(q, plane):
        at = lax.rem(q, PIECE)
        return ((at // 2) * 2 + q // PIECE, plane * 2 + lax.rem(at, 2))

    key_plane = lax.rem(row + 14, 16) // 2
    key_source = lax.rem(z * 2 + core + 2, 16)
    is_source = col == 0
    is_couple = jnp.logical_and(is_source, row == 1)

    barrier = pltpu.get_barrier_semaphore()

    def greet(dev):
        pl.semaphore_signal(barrier, inc=1, device_id=dev, device_id_type=MESH)

    def greet_plane(q, carry):
        @pl.when(q != my_piece)
        def _():
            greet(plane_device(q, z))

        return carry

    lax.fori_loop(0, 2 * PIECE, greet_plane, 0)
    greet(ring_dev[0])
    greet(ring_dev[1])

    @pl.when(z != 0)
    def _():
        greet((key_source, 0))
        greet((row, y))

    from_keys = jnp.where(jnp.logical_and(is_source, key_plane != 0), 16, 0)
    from_couple = jnp.where(z == 0, 7, 0)
    pl.semaphore_wait(barrier, 33 + from_keys + from_couple)

    load_own.wait()

    def is_shared(unit):
        return isinstance(unit, int) and unit == 3

    def ring_ref(d, s, unit):
        place = lax.rem(z + 8 - s, 8) if d == 0 else lax.rem(z + s, 8)
        return shared.at[place] if is_shared(unit) else own.at[place, unit]

    def ring_copy(d, s, unit, half):
        ref = ring_ref(d, s, unit)
        if half:
            rows = (SHARED if is_shared(unit) else TILE) // 2
            ref = ref.at[pl.ds(d * rows, rows)]
        return pltpu.make_async_remote_copy(
            ref, ref, ring_send.at[d, s, unit], ring_recv.at[d, s, unit],
            device_id=ring_dev[d], device_id_type=MESH,
        )

    def arrived(d, s, unit, half=False):
        ref = ring_ref(d, s, unit)
        if half:
            rows = (SHARED if is_shared(unit) else TILE) // 2
            ref = ref.at[pl.ds(d * rows, rows)]
        pltpu.make_async_remote_copy(
            ref, ref, ring_send.at[d, s - 1, unit], ring_recv.at[d, s - 1, unit],
            device_id=ring_dev[d], device_id_type=MESH,
        ).wait_recv()

    def mate_copy(unit):
        if unit == 3:
            ref, dst = own.at[z, 2, pl.ds(plain, SHARED)], shared.at[z]
        elif unit == 2:
            ref, dst = own.at[z, 2, pl.ds(0, plain)], mate.at[2, pl.ds(0, plain)]
        else:
            ref, dst = own.at[z, unit], mate.at[unit]
        return pltpu.make_async_remote_copy(
            ref, dst, mate_send.at[unit], mate_recv.at[unit], device_id=mate_dev, device_id_type=MESH
        )

    key_tile = jnp.where(row < 2, 1, 0)

    @pl.when(is_couple)
    def _():
        def send(q, carry):
            src = own.at[0, 0, pl.ds(lax.rem(q, PIECE) * 16, 16), pl.ds((q // PIECE) * 128, 128)]
            dst = pieces.at[q, :, pl.ds(512, 128)]

            @pl.when(q != my_piece)
            def _():
                pltpu.make_async_remote_copy(
                    src, dst, piece_sem.at[2], piece_sem.at[3], device_id=plane_device(q, 0), device_id_type=MESH
                ).start()

            @pl.when(q == my_piece)
            def _():
                pltpu.make_async_copy(src, dst, piece_sem.at[3]).start()

            return carry

        lax.fori_loop(0, 2 * PIECE, send, 0)

    @pl.when(is_source)
    def _():
        def send(p, carry):
            q = core * PIECE + p
            src = own.at[0, key_tile, pl.ds(p * 16, 16)]
            dst = pieces.at[q, :, pl.ds(0, 512)]
            itself = jnp.logical_and(key_plane == 0, q == my_piece)

            @pl.when(jnp.logical_not(itself))
            def _():
                pltpu.make_async_remote_copy(
                    src, dst, piece_sem.at[0], piece_sem.at[1], device_id=plane_device(q, key_plane),
                    device_id_type=MESH,
                ).start()

            @pl.when(itself)
            def _():
                pltpu.make_async_copy(src, dst, piece_sem.at[1]).start()

            return carry

        lax.fori_loop(0, PIECE, send, 0)

    for unit in (3, 0, 1, 2):
        mate_copy(unit).start()
        if unit != 3:
            for d in (0, 1):
                ring_copy(d, 0, unit, False).start()

    mine = pieces.at[my_piece]
    pltpu.make_async_copy(mine.at[:, pl.ds(512, 128)], mine.at[:, pl.ds(512, 128)], piece_sem.at[3]).wait()

    @pl.when(z == 0)
    def _():
        def send(i, carry):
            ref = mine.at[:, pl.ds(512, 128)]
            pltpu.make_async_remote_copy(
                ref, ref, piece_sem.at[4], piece_sem.at[3], device_id=(row, (i + 1) * 2 + y), device_id_type=MESH
            ).start()
            return carry

        lax.fori_loop(0, 7, send, 0)

    mate_copy(3).wait_recv()
    for d in (0, 1):
        ring_copy(d, 0, 3, False).start()

    pltpu.make_async_copy(mine.at[:, pl.ds(0, 512)], mine.at[:, pl.ds(0, 512)], piece_sem.at[1]).wait()

    def spread(q, carry):
        @pl.when(q != my_piece)
        def _():
            pltpu.make_async_remote_copy(
                mine, mine, spread_send, spread_recv, device_id=plane_device(q, z), device_id_type=MESH
            ).start()

        return carry

    lax.fori_loop(0, 2 * PIECE, spread, 0)

    for unit in (0, 1, 2):
        for d in (0, 1):
            arrived(d, 1, unit)
            ring_copy(d, 1, unit, False).start()

    peers = 2 * PIECE - 1
    pltpu.make_async_copy(pieces.at[pl.ds(0, peers)], pieces.at[pl.ds(0, peers)], spread_recv).wait()

    for part in (0, 1):
        raw = pieces[part * PIECE:(part + 1) * PIECE, :, 512:640].reshape(TILE, 128)
        keys[0, :, part * 128:(part + 1) * 128] = raw
    couple[...] = times_transposed(keys[0, :, 0:TILE], inverses[0]).astype(jnp.bfloat16)

    def factor(raw):
        left = times_transposed(raw[:, 0:TILE], inverses[0]).astype(jnp.bfloat16)
        reduced = (raw[:, TILE:].astype(jnp.float32) - times_transposed(left, couple[...])).astype(jnp.bfloat16)
        right = times_transposed(reduced, inverses[1]).astype(jnp.bfloat16)
        return left, right

    def product(factors, which):
        left, right = factors
        return times_transposed(left, keys[which, :, 0:TILE]) + times_transposed(right, keys[which, :, TILE:])

    for which in (0, 1):
        parity = y if which == 0 else 1 - y
        raw = pieces[pl.ds(parity * PIECE, PIECE), :, 0:512].reshape(TILE, 2 * TILE)
        left, right = factor(raw)
        keys[which, :, 0:TILE] = left
        keys[which, :, TILE:] = right

    load_window.wait()

    def subtract(tile, start, rows, amount):
        at = (tile, pl.ds(start, rows))
        window[at] = (window[at].astype(jnp.float32) - amount.astype(jnp.float32)).astype(jnp.bfloat16)
        pltpu.make_async_copy(window.at[at], updated.at[at], out_sem).start()

    def own_tile(place, unit):
        return (place * 2 + y) * 3 + unit

    def mate_tile(place, unit):
        return (place * 2 + 1 - y) * 3 + unit

    def local_tile(unit, carry):
        subtract(own_tile(z, unit), 0, TILE, product(factor(own[z, unit]), 0))
        return carry

    lax.fori_loop(0, 3, local_tile, 0)
    for unit in (0, 1):
        mate_copy(unit).wait_recv()
        subtract(mate_tile(z, unit), 0, TILE, product(factor(mate[unit]), 0))
    mate_copy(2).wait_recv()
    subtract(mate_tile(z, 2), 0, plain, product(factor(mate[2, 0:plain]), 0))
    subtract(mate_tile(z, 2), plain, SHARED, product(factor(shared[z]), 0))

    def place_of(d, s):
        return lax.rem(z + jnp.where(d == 0, 8 - s, s), 8)

    def sum_copy(place, unit, rows):
        return pltpu.make_async_remote_copy(
            sums_out.at[place, unit, pl.ds(0, rows)], sums_in.at[place, unit, pl.ds(0, rows)],
            sum_send.at[place, unit], sum_recv.at[place, unit], device_id=mate_dev, device_id_type=MESH,
        )

    def column_tile(place, unit):
        factors = factor(own[place, unit])
        sums_out[place, unit] = product(factors, 1).astype(jnp.bfloat16)

        @pl.when(unit != 2)
        def _():
            sum_copy(place, unit, TILE).start()

        @pl.when(unit == 2)
        def _():
            sum_copy(place, unit, plain).start()

        subtract(own_tile(place, unit), 0, TILE, product(factors, 0))

    def finish(place, unit):
        @pl.when(unit != 2)
        def _():
            sum_copy(place, unit, TILE).wait_recv()
            subtract(mate_tile(place, unit), 0, TILE, sums_in[place, unit])

        @pl.when(unit == 2)
        def _():
            sum_copy(place, unit, plain).wait_recv()
            subtract(mate_tile(place, unit), 0, plain, sums_in[place, unit, 0:plain])

    def shared_tile(place):
        subtract(mate_tile(place, 2), plain, SHARED, product(factor(shared[place]), 0))

    def pair(i, compute):
        s, unit = i // 3 + 1, lax.rem(i, 3)

        def one(d, carry):
            compute(place_of(d, s), unit)
            return carry

        lax.fori_loop(0, 2, one, 0)

    def visit(i, carry):
        s, unit = i // 3 + 1, lax.rem(i, 3)

        @pl.when(s > 1)
        def _():
            for d in (0, 1):
                arrived(d, s, unit)

                @pl.when(s == 2)
                def _():
                    ring_copy(d, s, unit, False).start()

                @pl.when(s == 3)
                def _():
                    ring_copy(d, s, unit, True).start()

        pair(i, column_tile)

        @pl.when(i > 0)
        def _():
            pair(i - 1, finish)

        @pl.when(unit == 2)
        def _():
            for d in (0, 1):
                arrived(d, s, 3)

                @pl.when(s < 3)
                def _():
                    ring_copy(d, s, 3, False).start()

                @pl.when(s == 3)
                def _():
                    ring_copy(d, s, 3, True).start()

            def one(d, carry):
                shared_tile(place_of(d, s))
                return carry

            lax.fori_loop(0, 2, one, 0)

        return carry

    lax.fori_loop(0, 9, visit, 0)

    far = lax.rem(z + 4, 8)

    def last(unit, carry):
        for d in (0, 1):
            arrived(d, 4, unit, True)
        column_tile(far, unit)

        @pl.when(unit == 0)
        def _():
            pair(8, finish)

        @pl.when(unit > 0)
        def _():
            finish(far, unit - 1)

        return carry

    lax.fori_loop(0, 3, last, 0)
    for d in (0, 1):
        arrived(d, 4, 3, True)
    shared_tile(far)
    finish(far, 2)

    for unit in range(4):
        mate_copy(unit).wait_send()
        for d in (0, 1):
            for s in range(4):
                ring_copy(d, s, unit, s == 3).wait_send()

    def drain(i, carry):
        place = lax.rem(z + i, 8)
        for unit in range(3):
            sum_copy(place, unit, plain if unit == 2 else TILE).wait_send()
        return carry

    lax.fori_loop(1, 8, drain, 0)
    pltpu.make_async_copy(pieces.at[pl.ds(0, peers)], pieces.at[pl.ds(0, peers)], spread_send).wait()

    @pl.when(z == 0)
    def _():
        ref = pieces.at[pl.ds(0, 7), :, pl.ds(512, 128)]
        pltpu.make_async_copy(ref, ref, piece_sem.at[4]).wait()

    @pl.when(is_source)
    def _():
        @pl.when(key_plane == 0)
        def _():
            ref = own.at[0, 0, pl.ds(0, 240)]
            pltpu.make_async_copy(ref, ref, piece_sem.at[0]).wait()

        @pl.when(key_plane != 0)
        def _():
            ref = own.at[0, 0]
            pltpu.make_async_copy(ref, ref, piece_sem.at[0]).wait()

    @pl.when(is_couple)
    def _():
        ref = pieces.at[pl.ds(0, peers), :, pl.ds(512, 128)]
        pltpu.make_async_copy(ref, ref, piece_sem.at[2]).wait()

    pltpu.make_async_copy(window, updated, out_sem).wait()


def shards(panel_cols, inverses, trailing):
    bf16 = jnp.bfloat16
    return pl.pallas_call(
        kernel,
        out_shape=jax.ShapeDtypeStruct(trailing.shape, bf16),
        in_specs=[
            pl.BlockSpec(memory_space=pl.ANY),
            pl.BlockSpec(memory_space=pltpu.VMEM),
            pl.BlockSpec(memory_space=pl.ANY),
        ],
        out_specs=pl.BlockSpec(memory_space=pl.ANY),
        scratch_shapes=[
            pltpu.VMEM((8, 3, TILE, 2 * TILE), bf16),
            pltpu.VMEM((3, TILE, 2 * TILE), bf16),
            pltpu.VMEM((8, SHARED, 2 * TILE), bf16),
            pltpu.VMEM((8, 3, TILE, TILE), bf16),
            pltpu.VMEM((8, 3, TILE, TILE), bf16),
            pltpu.VMEM((48, TILE, TILE), bf16),
            pltpu.VMEM((2 * PIECE, 16, 640), bf16),
            pltpu.VMEM((TILE, TILE), bf16),
            pltpu.VMEM((2, TILE, 2 * TILE), bf16),
            pltpu.SemaphoreType.DMA((2, 4, 4)),
            pltpu.SemaphoreType.DMA((2, 4, 4)),
            pltpu.SemaphoreType.DMA((4,)),
            pltpu.SemaphoreType.DMA((4,)),
            pltpu.SemaphoreType.DMA((8, 3)),
            pltpu.SemaphoreType.DMA((8, 3)),
            pltpu.SemaphoreType.DMA((2,)),
            pltpu.SemaphoreType.DMA((5,)),
            pltpu.SemaphoreType.DMA,
            pltpu.SemaphoreType.DMA,
            pltpu.SemaphoreType.DMA,
        ],
        compiler_params=pltpu.CompilerParams(
            collective_id=0, has_side_effects=True, vmem_limit_bytes=56 << 20
        ),
        name="panel_update",
    )(panel_cols, inverses, trailing)


def solution(mesh):
    in_specs = (P("col", "row", None), P(), P(None, "row", "col"))
    out_specs = P(None, "row", "col")
    return jax.shard_map(shards, mesh=mesh, in_specs=in_specs, out_specs=out_specs, check_vma=False)
```

time: 692 us -> 110 us (0.16)
  waiting for transfers between devices: 658 us -> 0 us
  Pallas kernels: 0 us -> 102 us
  matrix products: 15.6 us -> 0 us
  between operations: 13.2 us -> 0.01 us
    psum x2 -> x0, waiting for transfers between devices: 396 us -> none  [broadcast(): return lax.psum(kept, axis)]
    all_gather x1 -> x0, waiting for transfers between devices: 262 us -> none  [shards(): whole_panel = lax.all_gather(factored, 'col', axis=0, tiled=True)]
    pallas_call x0 -> x1, Pallas kernels: none -> 102 us  [shards(): pl.pallas_call(kernel, out_shape=jax.ShapeDtypeStruct(trailing.shape, bf1...]
    dot_general x3 -> x0, matrix products: 15.6 us -> none  [the longest x1 12.6 us: shards(): jnp.einsum('tak,bk->tab', whole_panel, key_tile, preferred_element_type=j...]
  transfers between devices with their start and end apart: 3 -> 0, of which waited for: 3 -> 0; matrix products, arithmetic and copies ran while one was open for 0% -> 0% of each run, Pallas kernels for 0% -> 0%
where the time goes in v1:
time: 110 us; the launch traced here: 108 us
  Pallas kernels  102 us (93%)
  local copies, waits for them, and re-layouts  6.2 us (6%)
    pallas_call x1, Pallas kernels, shards(): pl.pallas_call(kernel, out_shape=jax.ShapeDtypeStruct(trailing.shape, bf1...  102 us
    unnamed x1, local copies, waits for them, and re-layouts  6.2 us

profile of v1, /device:TPU:8, one launch (start us, length us, event | category | flops | bytes accessed | tf_op | source)
XLA Modules:
  0.0 107.8 jit_solution(449959974600699588)
XLA Ops:
  0.0 101.6 %panel_update.1 = bf16[48,256,256]{2,1,0:T(8,128)(2,1)} custom-call(bf16[3,256,512]{2,1,0:T(8,128)(2,1)} %panel.1, bf16[2,256,256]{2,1,0:T(8,128)(2,1)} %inverses.1, bf16[48,256,256]{2,1,0:T(8,128)(2,1)} %trailing.1), custom_call_target="tpu_custom_call" | custom-call | tf_op jit(solution)/shard_map/panel_update/pallas_call | solution.py:406
  101.6 6.2 %copy.5 = bf16[48,256,256]{2,1,0:T(8,128)(2,1)} copy(bf16[48,256,256]{2,1,0:T(8,128)(2,1)} %panel_update.1) | data formatting | bytes 12582912

commit v2 on v1

--- a/solution.py
+++ b/solution.py
@@ -18,10 +18,10 @@
 
 
 def kernel(
-    panel, inverses, trailing, updated,
-    own, mate, shared, sums_in, sums_out, window, pieces, couple, keys,
+    panel, inverses, trailing, window,
+    own, mate, shared, sums_in, sums_out, stage, couple_piece, pieces, couple, keys,
     ring_send, ring_recv, mate_send, mate_recv, sum_send, sum_recv,
-    load_sem, piece_sem, spread_send, spread_recv, out_sem,
+    load_sem, piece_sem, spread_send, spread_recv,
 ):
     row, col = lax.axis_index("row"), lax.axis_index("col")
     z, y = col // 2, lax.rem(col, 2)
@@ -41,7 +41,6 @@
         return ((at // 2) * 2 + q // PIECE, plane * 2 + lax.rem(at, 2))
 
     key_plane = lax.rem(row + 14, 16) // 2
-    key_source = lax.rem(z * 2 + core + 2, 16)
     is_source = col == 0
     is_couple = jnp.logical_and(is_source, row == 1)
 
@@ -63,12 +62,9 @@
 
     @pl.when(z != 0)
     def _():
-        greet((key_source, 0))
         greet((row, y))
 
-    from_keys = jnp.where(jnp.logical_and(is_source, key_plane != 0), 16, 0)
-    from_couple = jnp.where(z == 0, 7, 0)
-    pl.semaphore_wait(barrier, 33 + from_keys + from_couple)
+    pl.semaphore_wait(barrier, 33 + jnp.where(z == 0, 7, 0))
 
     load_own.wait()
 
@@ -116,17 +112,17 @@
     def _():
         def send(q, carry):
             src = own.at[0, 0, pl.ds(lax.rem(q, PIECE) * 16, 16), pl.ds((q // PIECE) * 128, 128)]
-            dst = pieces.at[q, :, pl.ds(512, 128)]
 
             @pl.when(q != my_piece)
             def _():
                 pltpu.make_async_remote_copy(
-                    src, dst, piece_sem.at[2], piece_sem.at[3], device_id=plane_device(q, 0), device_id_type=MESH
+                    src, couple_piece, piece_sem.at[2], piece_sem.at[3], device_id=plane_device(q, 0),
+                    device_id_type=MESH,
                 ).start()
 
             @pl.when(q == my_piece)
             def _():
-                pltpu.make_async_copy(src, dst, piece_sem.at[3]).start()
+                pltpu.make_async_copy(src, couple_piece, piece_sem.at[3]).start()
 
             return carry
 
@@ -137,17 +133,15 @@
         def send(p, carry):
             q = core * PIECE + p
             src = own.at[0, key_tile, pl.ds(p * 16, 16)]
-            dst = pieces.at[q, :, pl.ds(0, 512)]
-            itself = jnp.logical_and(key_plane == 0, q == my_piece)
-
-            @pl.when(jnp.logical_not(itself))
+            dst = stage.at[key_plane, :, pl.ds(0, 512)]
+
+            @pl.when(q != my_piece)
             def _():
                 pltpu.make_async_remote_copy(
-                    src, dst, piece_sem.at[0], piece_sem.at[1], device_id=plane_device(q, key_plane),
-                    device_id_type=MESH,
+                    src, dst, piece_sem.at[0], piece_sem.at[1], device_id=plane_device(q, 0), device_id_type=MESH
                 ).start()
 
-            @pl.when(itself)
+            @pl.when(q == my_piece)
             def _():
                 pltpu.make_async_copy(src, dst, piece_sem.at[1]).start()
 
@@ -162,24 +156,32 @@
                 ring_copy(d, 0, unit, False).start()
 
     mine = pieces.at[my_piece]
-    pltpu.make_async_copy(mine.at[:, pl.ds(512, 128)], mine.at[:, pl.ds(512, 128)], piece_sem.at[3]).wait()
 
     @pl.when(z == 0)
     def _():
-        def send(i, carry):
-            ref = mine.at[:, pl.ds(512, 128)]
+        staged = stage.at[:, :, pl.ds(0, 512)]
+        pltpu.make_async_copy(couple_piece, couple_piece, piece_sem.at[3]).wait()
+        pltpu.make_async_copy(staged, staged, piece_sem.at[1]).wait()
+        for plane in range(8):
+            stage[plane, :, 512:640] = couple_piece[...]
+
+        def send(plane, carry):
             pltpu.make_async_remote_copy(
-                ref, ref, piece_sem.at[4], piece_sem.at[3], device_id=(row, (i + 1) * 2 + y), device_id_type=MESH
+                stage.at[plane], mine, piece_sem.at[4], piece_sem.at[5], device_id=(row, plane * 2 + y),
+                device_id_type=MESH,
             ).start()
             return carry
 
-        lax.fori_loop(0, 7, send, 0)
+        lax.fori_loop(1, 8, send, 0)
+        pieces[my_piece] = stage[0]
 
     mate_copy(3).wait_recv()
     for d in (0, 1):
         ring_copy(d, 0, 3, False).start()
 
-    pltpu.make_async_copy(mine.at[:, pl.ds(0, 512)], mine.at[:, pl.ds(0, 512)], piece_sem.at[1]).wait()
+    @pl.when(z != 0)
+    def _():
+        pltpu.make_async_copy(mine, mine, piece_sem.at[5]).wait()
 
     def spread(q, carry):
         @pl.when(q != my_piece)
@@ -227,7 +229,6 @@
     def subtract(tile, start, rows, amount):
         at = (tile, pl.ds(start, rows))
         window[at] = (window[at].astype(jnp.float32) - amount.astype(jnp.float32)).astype(jnp.bfloat16)
-        pltpu.make_async_copy(window.at[at], updated.at[at], out_sem).start()
 
     def own_tile(place, unit):
         return (place * 2 + y) * 3 + unit
@@ -235,17 +236,13 @@
     def mate_tile(place, unit):
         return (place * 2 + 1 - y) * 3 + unit
 
-    def local_tile(unit, carry):
+    for unit in (0, 1, 2):
+        mate_copy(unit).wait_recv()
+    mate[2, plain:TILE] = shared[z]
+
+    def local_tile(unit):
         subtract(own_tile(z, unit), 0, TILE, product(factor(own[z, unit]), 0))
-        return carry
-
-    lax.fori_loop(0, 3, local_tile, 0)
-    for unit in (0, 1):
-        mate_copy(unit).wait_recv()
         subtract(mate_tile(z, unit), 0, TILE, product(factor(mate[unit]), 0))
-    mate_copy(2).wait_recv()
-    subtract(mate_tile(z, 2), 0, plain, product(factor(mate[2, 0:plain]), 0))
-    subtract(mate_tile(z, 2), plain, SHARED, product(factor(shared[z]), 0))
 
     def place_of(d, s):
         return lax.rem(z + jnp.where(d == 0, 8 - s, s), 8)
@@ -311,6 +308,10 @@
 
         pair(i, column_tile)
 
+        @pl.when(s == 2)
+        def _():
+            local_tile(unit)
+
         @pl.when(i > 0)
         def _():
             pair(i - 1, finish)
@@ -378,47 +379,39 @@
 
     @pl.when(z == 0)
     def _():
-        ref = pieces.at[pl.ds(0, 7), :, pl.ds(512, 128)]
+        ref = pieces.at[pl.ds(0, 7)]
         pltpu.make_async_copy(ref, ref, piece_sem.at[4]).wait()
 
     @pl.when(is_source)
     def _():
-        @pl.when(key_plane == 0)
-        def _():
-            ref = own.at[0, 0, pl.ds(0, 240)]
-            pltpu.make_async_copy(ref, ref, piece_sem.at[0]).wait()
-
-        @pl.when(key_plane != 0)
-        def _():
-            ref = own.at[0, 0]
-            pltpu.make_async_copy(ref, ref, piece_sem.at[0]).wait()
+        ref = own.at[0, 0, pl.ds(0, 240)]
+        pltpu.make_async_copy(ref, ref, piece_sem.at[0]).wait()
 
     @pl.when(is_couple)
     def _():
         ref = pieces.at[pl.ds(0, peers), :, pl.ds(512, 128)]
         pltpu.make_async_copy(ref, ref, piece_sem.at[2]).wait()
-
-    pltpu.make_async_copy(window, updated, out_sem).wait()
 
 
 def shards(panel_cols, inverses, trailing):
     bf16 = jnp.bfloat16
     return pl.pallas_call(
         kernel,
-        out_shape=jax.ShapeDtypeStruct(trailing.shape, bf16),
+        out_shape=pltpu.VMEM(trailing.shape, bf16),
         in_specs=[
             pl.BlockSpec(memory_space=pl.ANY),
             pl.BlockSpec(memory_space=pltpu.VMEM),
             pl.BlockSpec(memory_space=pl.ANY),
         ],
-        out_specs=pl.BlockSpec(memory_space=pl.ANY),
+        out_specs=pl.BlockSpec(memory_space=pltpu.VMEM),
         scratch_shapes=[
             pltpu.VMEM((8, 3, TILE, 2 * TILE), bf16),
             pltpu.VMEM((3, TILE, 2 * TILE), bf16),
             pltpu.VMEM((8, SHARED, 2 * TILE), bf16),
             pltpu.VMEM((8, 3, TILE, TILE), bf16),
             pltpu.VMEM((8, 3, TILE, TILE), bf16),
-            pltpu.VMEM((48, TILE, TILE), bf16),
+            pltpu.VMEM((8, 16, 640), bf16),
+            pltpu.VMEM((16, 128), bf16),
             pltpu.VMEM((2 * PIECE, 16, 640), bf16),
             pltpu.VMEM((TILE, TILE), bf16),
             pltpu.VMEM((2, TILE, 2 * TILE), bf16),
@@ -429,8 +422,7 @@
             pltpu.SemaphoreType.DMA((8, 3)),
             pltpu.SemaphoreType.DMA((8, 3)),
             pltpu.SemaphoreType.DMA((2,)),
-            pltpu.SemaphoreType.DMA((5,)),
-            pltpu.SemaphoreType.DMA,
+            pltpu.SemaphoreType.DMA((6,)),
             pltpu.SemaphoreType.DMA,
             pltpu.SemaphoreType.DMA,
         ],

time: 110 us -> 98.2 us (0.89); the launches traced: 108 us -> 98.1 us
  Pallas kernels: 102 us -> 95.4 us
  local copies, waits for them, and re-layouts: 6.2 us -> 2.71 us
    pallas_call x1, Pallas kernels: 102 us -> 95.4 us  [shards(): pl.pallas_call(kernel, out_shape=pltpu.VMEM(trailing.shape, bf16), in_spe...]
    unnamed x1, local copies, waits for them, and re-layouts: 6.2 us -> 2.71 us
where the time goes in v2:
time: 98.2 us; the launch traced here: 98.1 us
  Pallas kernels  95.4 us (97%)
  local copies, waits for them, and re-layouts  2.71 us (3%)
    pallas_call x1, Pallas kernels, shards(): pl.pallas_call(kernel, out_shape=pltpu.VMEM(trailing.shape, bf16), in_spe...  95.4 us
    unnamed x1, local copies, waits for them, and re-layouts  2.71 us

profile of v2, /device:TPU:8, one launch (start us, length us, event | category | flops | bytes accessed | tf_op | source)
XLA Modules:
  0.0 98.1 jit_solution(10117731384238007431)
XLA Ops:
  0.0 95.4 %panel_update.1 = bf16[48,256,256]{2,1,0:T(8,128)(2,1)S(1)} custom-call(bf16[3,256,512]{2,1,0:T(8,128)(2,1)} %panel.1, bf16[2,256,256]{2,1,0:T(8,128)(2,1)} %inverses.1, bf16[48,256,256]{2,1,0:T(8,128)(2,1)} %trailing.1), custom_call_target="tpu_custom_call" | custom-call | tf_op jit(solution)/shard_map/panel_update/pallas_call | solution.py:398
  95.4 2.7 %copy.5 = bf16[48,256,256]{2,1,0:T(8,128)(2,1)} copy(bf16[48,256,256]{2,1,0:T(8,128)(2,1)S(1)} %panel_update.1) | data formatting | bytes 12582912

commit v3 on v2

--- a/solution.py
+++ b/solution.py
@@ -10,6 +10,8 @@
 MESH = pl.DeviceIdType.MESH
 TILE = 256
 SHARED = 128
+FIRST = (0,)
+FORWARD_FIRST = True
 PIECE = 16
 
 
@@ -21,13 +23,14 @@
     panel, inverses, trailing, window,
     own, mate, shared, sums_in, sums_out, stage, couple_piece, pieces, couple, keys,
     ring_send, ring_recv, mate_send, mate_recv, sum_send, sum_recv,
-    load_sem, piece_sem, spread_send, spread_recv,
+    load_sem, piece_sem, spread_sem, ready_sem,
 ):
     row, col = lax.axis_index("row"), lax.axis_index("col")
     z, y = col // 2, lax.rem(col, 2)
     chip, core = row // 2, lax.rem(row, 2)
     my_piece = core * PIECE + chip * 2 + y
     mate_dev = (row, col + 1 - 2 * y)
+    core_dev = (row + 1 - 2 * core, col)
     ring_dev = ((row, lax.rem(col + 2, 16)), (row, lax.rem(col + 14, 16)))
     plain = TILE - SHARED
 
@@ -49,22 +52,45 @@
     def greet(dev):
         pl.semaphore_signal(barrier, inc=1, device_id=dev, device_id_type=MESH)
 
-    def greet_plane(q, carry):
-        @pl.when(q != my_piece)
-        def _():
-            greet(plane_device(q, z))
+    def greet_plane(p, carry):
+        @pl.when(core * PIECE + p != my_piece)
+        def _():
+            greet(plane_device(core * PIECE + p, z))
 
         return carry
 
-    lax.fori_loop(0, 2 * PIECE, greet_plane, 0)
-    greet(ring_dev[0])
-    greet(ring_dev[1])
+    lax.fori_loop(0, PIECE, greet_plane, 0)
+    greet(core_dev)
+
+    @pl.when(jnp.logical_and(jnp.logical_and(z == 0, core == 0), row + col > 0))
+    def _():
+        greet((1, 0))
+
+    @pl.when(z == 0)
+    def _():
+        def greet_place(place, carry):
+            greet((row, place * 2 + y))
+            return carry
+
+        lax.fori_loop(1, 8, greet_place, 0)
+
+    @pl.when(jnp.logical_and(z != 0, z != 7))
+    def _():
+        greet(ring_dev[0])
+
+    @pl.when(z > 1)
+    def _():
+        greet(ring_dev[1])
+
+    beside = jnp.logical_or(z == 1, z == 7)
+    from_others = jnp.where(z == 0, 0, jnp.where(beside, 2, 3))
+    pl.semaphore_wait(barrier, 16 + from_others + jnp.where(is_couple, 15, 0))
 
     @pl.when(z != 0)
     def _():
-        greet((row, y))
-
-    pl.semaphore_wait(barrier, 33 + jnp.where(z == 0, 7, 0))
+        pl.semaphore_signal(
+            ready_sem.at[jnp.where(beside, 0, 1)], inc=1, device_id=(row, y), device_id_type=MESH
+        )
 
     load_own.wait()
 
@@ -149,21 +175,41 @@
 
         lax.fori_loop(0, PIECE, send, 0)
 
+    def begin(units):
+        for unit in units:
+            for d in (0, 1):
+                ring_copy(d, 0, unit, False).start()
+
+    mine = pieces.at[my_piece]
+
+    def spread():
+        def send(p, carry):
+            q = core * PIECE + p
+
+            @pl.when(q != my_piece)
+            def _():
+                pltpu.make_async_remote_copy(
+                    mine, mine, spread_sem.at[0], spread_sem.at[1], device_id=plane_device(q, z), device_id_type=MESH
+                ).start()
+
+            return carry
+
+        lax.fori_loop(0, PIECE, send, 0)
+
     for unit in (3, 0, 1, 2):
         mate_copy(unit).start()
-        if unit != 3:
-            for d in (0, 1):
-                ring_copy(d, 0, unit, False).start()
-
-    mine = pieces.at[my_piece]
 
     @pl.when(z == 0)
     def _():
+        pl.semaphore_wait(ready_sem.at[0], 2)
+        begin(FIRST)
         staged = stage.at[:, :, pl.ds(0, 512)]
         pltpu.make_async_copy(couple_piece, couple_piece, piece_sem.at[3]).wait()
         pltpu.make_async_copy(staged, staged, piece_sem.at[1]).wait()
         for plane in range(8):
             stage[plane, :, 512:640] = couple_piece[...]
+        pieces[my_piece] = stage[0]
+        pl.semaphore_wait(ready_sem.at[1], 5)
 
         def send(plane, carry):
             pltpu.make_async_remote_copy(
@@ -173,34 +219,38 @@
             return carry
 
         lax.fori_loop(1, 8, send, 0)
-        pieces[my_piece] = stage[0]
+        spread()
+        begin([unit for unit in (0, 1, 2) if unit not in FIRST])
+
+    @pl.when(z != 0)
+    def _():
+        begin((0, 1, 2))
 
     mate_copy(3).wait_recv()
+    begin((3,))
+
+    @pl.when(z != 0)
+    def _():
+        pltpu.make_async_copy(mine, mine, piece_sem.at[5]).wait()
+        spread()
+
+    peers = pieces.at[pl.ds(0, PIECE - 1)]
+    half = pieces.at[pl.ds(core * PIECE, PIECE)]
+    swap = pltpu.make_async_remote_copy(
+        half, half, spread_sem.at[2], spread_sem.at[3], device_id=core_dev, device_id_type=MESH
+    )
+
     for d in (0, 1):
-        ring_copy(d, 0, 3, False).start()
-
-    @pl.when(z != 0)
-    def _():
-        pltpu.make_async_copy(mine, mine, piece_sem.at[5]).wait()
-
-    def spread(q, carry):
-        @pl.when(q != my_piece)
-        def _():
-            pltpu.make_async_remote_copy(
-                mine, mine, spread_send, spread_recv, device_id=plane_device(q, z), device_id_type=MESH
-            ).start()
-
-        return carry
-
-    lax.fori_loop(0, 2 * PIECE, spread, 0)
-
-    for unit in (0, 1, 2):
+        arrived(d, 1, 0)
+        ring_copy(d, 1, 0, False).start()
+    pltpu.make_async_copy(peers, peers, spread_sem.at[1]).wait()
+    swap.start()
+    for unit in (1, 2):
         for d in (0, 1):
-            arrived(d, 1, unit)
-            ring_copy(d, 1, unit, False).start()
-
-    peers = 2 * PIECE - 1
-    pltpu.make_async_copy(pieces.at[pl.ds(0, peers)], pieces.at[pl.ds(0, peers)], spread_recv).wait()
+            if FORWARD_FIRST:
+                arrived(d, 1, unit)
+                ring_copy(d, 1, unit, False).start()
+    swap.wait_recv()
 
     for part in (0, 1):
         raw = pieces[part * PIECE:(part + 1) * PIECE, :, 512:640].reshape(TILE, 128)
@@ -236,8 +286,6 @@
     def mate_tile(place, unit):
         return (place * 2 + 1 - y) * 3 + unit
 
-    for unit in (0, 1, 2):
-        mate_copy(unit).wait_recv()
     mate[2, plain:TILE] = shared[z]
 
     def local_tile(unit):
@@ -293,12 +341,12 @@
     def visit(i, carry):
         s, unit = i // 3 + 1, lax.rem(i, 3)
 
-        @pl.when(s > 1)
+        @pl.when(i >= (3 if FORWARD_FIRST else 1))
         def _():
             for d in (0, 1):
                 arrived(d, s, unit)
 
-                @pl.when(s == 2)
+                @pl.when(s < 3)
                 def _():
                     ring_copy(d, s, unit, False).start()
 
@@ -307,6 +355,11 @@
                     ring_copy(d, s, unit, True).start()
 
         pair(i, column_tile)
+
+        @pl.when(i == 3)
+        def _():
+            for u in (0, 1, 2):
+                mate_copy(u).wait_recv()
 
         @pl.when(s == 2)
         def _():
@@ -375,7 +428,8 @@
         return carry
 
     lax.fori_loop(1, 8, drain, 0)
-    pltpu.make_async_copy(pieces.at[pl.ds(0, peers)], pieces.at[pl.ds(0, peers)], spread_send).wait()
+    pltpu.make_async_copy(peers, peers, spread_sem.at[0]).wait()
+    swap.wait_send()
 
     @pl.when(z == 0)
     def _():
@@ -389,7 +443,7 @@
 
     @pl.when(is_couple)
     def _():
-        ref = pieces.at[pl.ds(0, peers), :, pl.ds(512, 128)]
+        ref = pieces.at[pl.ds(0, 2 * PIECE - 1), :, pl.ds(512, 128)]
         pltpu.make_async_copy(ref, ref, piece_sem.at[2]).wait()
 
 
@@ -423,8 +477,8 @@
             pltpu.SemaphoreType.DMA((8, 3)),
             pltpu.SemaphoreType.DMA((2,)),
             pltpu.SemaphoreType.DMA((6,)),
-            pltpu.SemaphoreType.DMA,
-            pltpu.SemaphoreType.DMA,
+            pltpu.SemaphoreType.DMA((4,)),
+            pltpu.SemaphoreType.REGULAR((2,)),
         ],
         compiler_params=pltpu.CompilerParams(
             collective_id=0, has_side_effects=True, vmem_limit_bytes=56 << 20

time: 98.2 us -> 93 us (0.947); the launches traced: 98.1 us -> 91.5 us
  Pallas kernels: 95.4 us -> 88.8 us
    pallas_call x1, Pallas kernels: 95.4 us -> 88.8 us  [shards(): pl.pallas_call(kernel, out_shape=pltpu.VMEM(trailing.shape, bf16), in_spe...]
where the time goes in v3:
time: 93 us; the launch traced here: 91.5 us
  Pallas kernels  88.8 us (95%)
  local copies, waits for them, and re-layouts  2.71 us (3%)
    pallas_call x1, Pallas kernels, shards(): pl.pallas_call(kernel, out_shape=pltpu.VMEM(trailing.shape, bf16), in_spe...  88.8 us
    unnamed x1, local copies, waits for them, and re-layouts  2.71 us

profile of v3, /device:TPU:8, one launch (start us, length us, event | category | flops | bytes accessed | tf_op | source)
XLA Modules:
  0.0 91.5 jit_solution(6740802667928295284)
XLA Ops:
  0.0 88.8 %panel_update.1 = bf16[48,256,256]{2,1,0:T(8,128)(2,1)S(1)} custom-call(bf16[3,256,512]{2,1,0:T(8,128)(2,1)} %panel.1, bf16[2,256,256]{2,1,0:T(8,128)(2,1)} %inverses.1, bf16[48,256,256]{2,1,0:T(8,128)(2,1)} %trailing.1), custom_call_target="tpu_custom_call" | custom-call | tf_op jit(solution)/shard_map/panel_update/pallas_call | solution.py:452
  88.8 2.7 %copy.5 = bf16[48,256,256]{2,1,0:T(8,128)(2,1)} copy(bf16[48,256,256]{2,1,0:T(8,128)(2,1)S(1)} %panel_update.1) | data formatting | bytes 12582912

commit v4 on v3

--- a/solution.py
+++ b/solution.py
@@ -10,8 +10,9 @@
 MESH = pl.DeviceIdType.MESH
 TILE = 256
 SHARED = 128
-FIRST = (0,)
-FORWARD_FIRST = True
+FIRST = 128
+FEWER = 64
+BEFORE = (3, 0)
 PIECE = 16
 
 
@@ -101,31 +102,46 @@
         place = lax.rem(z + 8 - s, 8) if d == 0 else lax.rem(z + s, 8)
         return shared.at[place] if is_shared(unit) else own.at[place, unit]
 
-    def ring_copy(d, s, unit, half):
+    def ring_copy(d, s, unit, up=None):
         ref = ring_ref(d, s, unit)
-        if half:
-            rows = (SHARED if is_shared(unit) else TILE) // 2
-            ref = ref.at[pl.ds(d * rows, rows)]
+        if up is not None:
+            rows = SHARED if is_shared(unit) else TILE
+            up = up * rows // TILE
+            ref = ref.at[pl.ds(0, up)] if d == 0 else ref.at[pl.ds(up, rows - up)]
         return pltpu.make_async_remote_copy(
             ref, ref, ring_send.at[d, s, unit], ring_recv.at[d, s, unit],
             device_id=ring_dev[d], device_id_type=MESH,
         )
 
-    def arrived(d, s, unit, half=False):
+    def arrived(d, s, unit, up=None):
         ref = ring_ref(d, s, unit)
-        if half:
-            rows = (SHARED if is_shared(unit) else TILE) // 2
-            ref = ref.at[pl.ds(d * rows, rows)]
+        if up is not None:
+            rows = SHARED if is_shared(unit) else TILE
+            up = up * rows // TILE
+            ref = ref.at[pl.ds(0, up)] if d == 0 else ref.at[pl.ds(up, rows - up)]
         pltpu.make_async_remote_copy(
             ref, ref, ring_send.at[d, s - 1, unit], ring_recv.at[d, s - 1, unit],
             device_id=ring_dev[d], device_id_type=MESH,
         ).wait_recv()
 
+    def opposite(place, action):
+        @pl.when(place == 1)
+        def _():
+            action(FEWER)
+
+        @pl.when(place == 7)
+        def _():
+            action(TILE - FEWER)
+
+        @pl.when(jnp.logical_and(place != 1, place != 7))
+        def _():
+            action(TILE // 2)
+
+    next_place = (lax.rem(z + 1, 8), lax.rem(z + 7, 8))
+
     def mate_copy(unit):
         if unit == 3:
             ref, dst = own.at[z, 2, pl.ds(plain, SHARED)], shared.at[z]
-        elif unit == 2:
-            ref, dst = own.at[z, 2, pl.ds(0, plain)], mate.at[2, pl.ds(0, plain)]
         else:
             ref, dst = own.at[z, unit], mate.at[unit]
         return pltpu.make_async_remote_copy(
@@ -178,7 +194,15 @@
     def begin(units):
         for unit in units:
             for d in (0, 1):
-                ring_copy(d, 0, unit, False).start()
+                ring_copy(d, 0, unit).start()
+
+    def begin_part(start, rows):
+        if rows:
+            for d in (0, 1):
+                ref = own.at[z, 0, pl.ds(start, rows)]
+                pltpu.make_async_remote_copy(
+                    ref, ref, ring_send.at[d, 0, 0], ring_recv.at[d, 0, 0], device_id=ring_dev[d], device_id_type=MESH
+                ).start()
 
     mine = pieces.at[my_piece]
 
@@ -195,14 +219,17 @@
             return carry
 
         lax.fori_loop(0, PIECE, send, 0)
-
-    for unit in (3, 0, 1, 2):
+        for unit in (0, 1):
+            if unit not in BEFORE:
+                mate_copy(unit).start()
+
+    for unit in BEFORE:
         mate_copy(unit).start()
 
     @pl.when(z == 0)
     def _():
         pl.semaphore_wait(ready_sem.at[0], 2)
-        begin(FIRST)
+        begin_part(0, FIRST)
         staged = stage.at[:, :, pl.ds(0, 512)]
         pltpu.make_async_copy(couple_piece, couple_piece, piece_sem.at[3]).wait()
         pltpu.make_async_copy(staged, staged, piece_sem.at[1]).wait()
@@ -219,8 +246,9 @@
             return carry
 
         lax.fori_loop(1, 8, send, 0)
+        begin_part(FIRST, TILE - FIRST)
+        begin((1, 2))
         spread()
-        begin([unit for unit in (0, 1, 2) if unit not in FIRST])
 
     @pl.when(z != 0)
     def _():
@@ -242,14 +270,13 @@
 
     for d in (0, 1):
         arrived(d, 1, 0)
-        ring_copy(d, 1, 0, False).start()
+        ring_copy(d, 1, 0).start()
     pltpu.make_async_copy(peers, peers, spread_sem.at[1]).wait()
     swap.start()
     for unit in (1, 2):
         for d in (0, 1):
-            if FORWARD_FIRST:
-                arrived(d, 1, unit)
-                ring_copy(d, 1, unit, False).start()
+            arrived(d, 1, unit)
+            ring_copy(d, 1, unit).start()
     swap.wait_recv()
 
     for part in (0, 1):
@@ -286,8 +313,6 @@
     def mate_tile(place, unit):
         return (place * 2 + 1 - y) * 3 + unit
 
-    mate[2, plain:TILE] = shared[z]
-
     def local_tile(unit):
         subtract(own_tile(z, unit), 0, TILE, product(factor(own[z, unit]), 0))
         subtract(mate_tile(z, unit), 0, TILE, product(factor(mate[unit]), 0))
@@ -341,46 +366,51 @@
     def visit(i, carry):
         s, unit = i // 3 + 1, lax.rem(i, 3)
 
-        @pl.when(i >= (3 if FORWARD_FIRST else 1))
+        @pl.when(s > 1)
         def _():
             for d in (0, 1):
                 arrived(d, s, unit)
 
+                @pl.when(s == 2)
+                def _():
+                    ring_copy(d, s, unit).start()
+
+                @pl.when(s == 3)
+                def _():
+                    opposite(next_place[d], lambda up: ring_copy(d, s, unit, up).start())
+
+        pair(i, column_tile)
+
+        @pl.when(i == 3)
+        def _():
+            mate_copy(0).wait_recv()
+            mate_copy(1).wait_recv()
+
+        @pl.when(jnp.logical_and(s == 2, unit != 2))
+        def _():
+            local_tile(unit)
+
+        @pl.when(i == 5)
+        def _():
+            finish(z, 2)
+            shared_tile(z)
+
+        @pl.when(i > 0)
+        def _():
+            pair(i - 1, finish)
+
+        @pl.when(unit == 2)
+        def _():
+            for d in (0, 1):
+                arrived(d, s, 3)
+
                 @pl.when(s < 3)
                 def _():
-                    ring_copy(d, s, unit, False).start()
+                    ring_copy(d, s, 3).start()
 
                 @pl.when(s == 3)
                 def _():
-                    ring_copy(d, s, unit, True).start()
-
-        pair(i, column_tile)
-
-        @pl.when(i == 3)
-        def _():
-            for u in (0, 1, 2):
-                mate_copy(u).wait_recv()
-
-        @pl.when(s == 2)
-        def _():
-            local_tile(unit)
-
-        @pl.when(i > 0)
-        def _():
-            pair(i - 1, finish)
-
-        @pl.when(unit == 2)
-        def _():
-            for d in (0, 1):
-                arrived(d, s, 3)
-
-                @pl.when(s < 3)
-                def _():
-                    ring_copy(d, s, 3, False).start()
-
-                @pl.when(s == 3)
-                def _():
-                    ring_copy(d, s, 3, True).start()
+                    opposite(next_place[d], lambda up: ring_copy(d, s, 3, up).start())
 
             def one(d, carry):
                 shared_tile(place_of(d, s))
@@ -390,13 +420,14 @@
 
         return carry
 
+    column_tile(z, 2)
     lax.fori_loop(0, 9, visit, 0)
 
     far = lax.rem(z + 4, 8)
 
     def last(unit, carry):
         for d in (0, 1):
-            arrived(d, 4, unit, True)
+            opposite(z, lambda up: arrived(d, 4, unit, up))
         column_tile(far, unit)
 
         @pl.when(unit == 0)
@@ -411,15 +442,17 @@
 
     lax.fori_loop(0, 3, last, 0)
     for d in (0, 1):
-        arrived(d, 4, 3, True)
+        opposite(z, lambda up: arrived(d, 4, 3, up))
     shared_tile(far)
     finish(far, 2)
 
     for unit in range(4):
-        mate_copy(unit).wait_send()
+        if unit != 2:
+            mate_copy(unit).wait_send()
         for d in (0, 1):
-            for s in range(4):
-                ring_copy(d, s, unit, s == 3).wait_send()
+            for s in range(3):
+                ring_copy(d, s, unit).wait_send()
+            opposite(next_place[d], lambda up: ring_copy(d, 3, unit, up).wait_send())
 
     def drain(i, carry):
         place = lax.rem(z + i, 8)
@@ -428,6 +461,7 @@
         return carry
 
     lax.fori_loop(1, 8, drain, 0)
+    sum_copy(z, 2, plain).wait_send()
     pltpu.make_async_copy(peers, peers, spread_sem.at[0]).wait()
     swap.wait_send()
 
@@ -460,7 +494,7 @@
         out_specs=pl.BlockSpec(memory_space=pltpu.VMEM),
         scratch_shapes=[
             pltpu.VMEM((8, 3, TILE, 2 * TILE), bf16),
-            pltpu.VMEM((3, TILE, 2 * TILE), bf16),
+            pltpu.VMEM((2, TILE, 2 * TILE), bf16),
             pltpu.VMEM((8, SHARED, 2 * TILE), bf16),
             pltpu.VMEM((8, 3, TILE, TILE), bf16),
             pltpu.VMEM((8, 3, TILE, TILE), bf16),

time: 93 us -> 90.1 us (0.969); the launches traced: 91.5 us -> 90 us
  Pallas kernels: 88.8 us -> 87.2 us
    pallas_call x1, Pallas kernels: 88.8 us -> 87.2 us  [shards(): pl.pallas_call(kernel, out_shape=pltpu.VMEM(trailing.shape, bf16), in_spe...]
where the time goes in v4:
time: 90.1 us; the launch traced here: 90 us
  Pallas kernels  87.2 us (97%)
  local copies, waits for them, and re-layouts  2.71 us (3%)
    pallas_call x1, Pallas kernels, shards(): pl.pallas_call(kernel, out_shape=pltpu.VMEM(trailing.shape, bf16), in_spe...  87.2 us
    unnamed x1, local copies, waits for them, and re-layouts  2.71 us

profile of v4, /device:TPU:8, one launch (start us, length us, event | category | flops | bytes accessed | tf_op | source)
XLA Modules:
  0.0 90.0 jit_solution(3182269666316263750)
XLA Ops:
  0.0 87.2 %panel_update.1 = bf16[48,256,256]{2,1,0:T(8,128)(2,1)S(1)} custom-call(bf16[3,256,512]{2,1,0:T(8,128)(2,1)} %panel.1, bf16[2,256,256]{2,1,0:T(8,128)(2,1)} %inverses.1, bf16[48,256,256]{2,1,0:T(8,128)(2,1)} %trailing.1), custom_call_target="tpu_custom_call" | custom-call | tf_op jit(solution)/shard_map/panel_update/pallas_call | solution.py:486
  87.3 2.7 %copy.5 = bf16[48,256,256]{2,1,0:T(8,128)(2,1)} copy(bf16[48,256,256]{2,1,0:T(8,128)(2,1)S(1)} %panel_update.1) | data formatting | bytes 12582912
